TPU v7x, 128 devices: a whole 4x4x4 slice. The times are simulated.
128 devices in a mesh: tm: 16 (over y, x), rows: 8 (over z, core).
Axes of the slice: x: 4, y: 4, z: 4, core: 2. Of those that a mesh axis runs over, the one named last changes fastest.
Arguments:
- observations: float32 [128, 1024], P('tm'), may hold values from -6 to 6
- observed: int32 [128], P('tm'), may hold values 0 or 1
- start_mean: float32 [1024], replicated, may hold values from -6 to 6
- transition: float32 [1024, 1024], P(('tm', 'rows')), may hold values from -1 to 1
- closed_loop: float32 [1024, 1024], P(('tm', 'rows')), may hold values from -1 to 1
- obs_gain: float32 [1024, 1024], replicated, may hold values from -0.0625 to 0.0625
- smooth_observed: float32 [1024, 1024], P(('tm', 'rows')), may hold values from -1 to 1
- smooth_missing: float32 [1024, 1024], P(('tm', 'rows')), may hold values from -1 to 1
Outputs:
- filtered: float32 [128, 1024], P('tm', 'rows')
- smoothed: float32 [128, 1024], P('tm', 'rows')
All inputs are finite; a program needn't handle non-finite values. No bound on the sum of `observed` on one device may be relied on, other than what follows from the above.
Results may differ from a plain program's by a relative error of at most 0.0003.
Values sent between devices are 32-bit elements; how exact they have to be, the bound alone decides.
No kernel may reach another device: no remote copies, remote signals or barrier semaphores. Data moves between devices by JAX's collectives and lax.ppermute only.
A program may use at most 128 MiB of HBM per device.

v0:
```python
from functools import partial
import jax
import jax.numpy as jnp
from jax import lax
from jax.sharding import PartitionSpec as P

precise_dot = partial(jnp.dot, precision=lax.Precision.HIGHEST)


def shifted(value, axis, steps):
    count = lax.axis_size(axis)
    initial, last = (max(0, -steps), min(count, count - steps))
    return lax.ppermute(value, axis, [(source, source + steps) for source in range(initial, last)])


def full_state(row_vec, direction):
    moved = shifted(row_vec, "tm", direction)
    return lax.all_gather(moved, "rows", axis=0, tiled=True)


def doubling_scan(matrix_rows, vector_rows, direction, segments):
    levels = (segments - 1).bit_length()
    for level_index in range(levels - 2):
        stride = direction * 2**level_index
        other_matrix, other_vector = shifted((matrix_rows, vector_rows), "tm", stride)
        start_totals = (
            jnp.zeros(matrix_rows.shape, jnp.float32),
            jnp.zeros(vector_rows.shape, jnp.float32),
        )
        pieces = (
            lax.all_gather(other_matrix, "rows", axis=0, tiled=True),
            lax.all_gather(other_vector, "rows", axis=0, tiled=True),
        )
        columns = lax.slice_in_dim(matrix_rows, 0, pieces[0].shape[0], axis=1)
        new_matrix = start_totals[0] + precise_dot(columns, pieces[0])
        new_vector = start_totals[1] + precise_dot(columns, pieces[1])
        matrix_rows, vector_rows = (new_matrix, vector_rows + new_vector)
    stride = direction * 2 ** max(levels - 2, 0)
    result_rows = vector_rows
    for repeat in range(3):
        result_rows = vector_rows + precise_dot(matrix_rows, full_state(result_rows, stride))
    return full_state(result_rows, direction)


def shards(
    observations,
    observed,
    start_mean,
    transition,
    closed_loop,
    obs_gain,
    smooth_observed,
    smooth_missing,
):
    seg_steps = observations.shape[0]
    state_dim = obs_gain.shape[0]
    segments = lax.axis_size("tm")
    row_count = state_dim // lax.axis_size("rows")
    seg_index = lax.axis_index("tm")
    row_start = lax.axis_index("rows") * row_count
    trans_full, closed_full, seen_full, missing_full = (
        lax.all_gather(transition, ("tm", "rows"), axis=0, tiled=True),
        lax.all_gather(closed_loop, ("tm", "rows"), axis=0, tiled=True),
        lax.all_gather(smooth_observed, ("tm", "rows"), axis=0, tiled=True),
        lax.all_gather(smooth_missing, ("tm", "rows"), axis=0, tiled=True),
    )
    dynamics = jnp.stack((trans_full, closed_full))
    seen_float = observed.astype(jnp.float32)
    inject = (
        lax.dot_general(
            observations, obs_gain, (((1,), (1,)), ((), ())), precision=lax.Precision.HIGHEST
        )
        * seen_float[:, None]
    )
    anchor = jnp.where(seg_index == 0, start_mean, jnp.zeros_like(start_mean))

    def forward_step(state_vec, inputs):
        is_seen, inject_row = inputs
        matrix = lax.dynamic_index_in_dim(dynamics, is_seen, 0, keepdims=False)
        state_vec = precise_dot(matrix, state_vec) + inject_row
        return (state_vec, state_vec)

    local_end = lax.scan(forward_step, anchor, (observed, inject))[0]
    row_ids = lax.broadcasted_iota(jnp.int32, (row_count, state_dim), 0) + row_start
    col_ids = lax.broadcasted_iota(jnp.int32, (row_count, state_dim), 1)
    eye_rows = (row_ids == col_ids).astype(jnp.float32)

    def compose_forward(product, is_seen):
        matrix = lax.dynamic_index_in_dim(dynamics, is_seen, 0, keepdims=False)
        return (precise_dot(product, matrix), None)

    forward_rows = lax.scan(compose_forward, eye_rows, observed, reverse=True)[0]
    forward_rows = forward_rows * (seg_index != 0).astype(jnp.float32)
    gains = jnp.stack((missing_full, seen_full))
    step_ids = lax.iota(jnp.int32, seg_steps) + seg_index * seg_steps
    keep_gain = (step_ids != segments * seg_steps - 1).astype(jnp.float32)

    def compose_backward(product, inputs):
        is_seen, keep_now = inputs
        matrix = lax.dynamic_index_in_dim(gains, is_seen, 0, keepdims=False)
        return (precise_dot(product, matrix) * keep_now, None)

    backward_rows = lax.scan(compose_backward, eye_rows, (observed, keep_gain))[0]
    end_rows = lax.dynamic_slice_in_dim(local_end, row_start, row_count)
    start_full = doubling_scan(forward_rows, end_rows, 1, segments) + anchor
    filtered_full = lax.scan(forward_step, start_full, (observed, inject))[1]
    predicted = lax.dot_general(
        filtered_full, trans_full, (((1,), (1,)), ((), ())), precision=lax.Precision.HIGHEST
    )

    def backward_step(state_vec, inputs):
        is_seen, keep_now, mean_row, predicted_row = inputs
        matrix = lax.dynamic_index_in_dim(gains, is_seen, 0, keepdims=False)
        state_vec = mean_row + keep_now * precise_dot(matrix, state_vec - predicted_row)
        return (state_vec, state_vec)

    backward_inputs = (observed, keep_gain, filtered_full, predicted)
    zero_state = jnp.zeros_like(start_mean)
    local_first = lax.scan(backward_step, zero_state, backward_inputs, reverse=True)[0]
    first_rows = lax.dynamic_slice_in_dim(local_first, row_start, row_count)
    next_full = doubling_scan(backward_rows, first_rows, -1, segments)
    smoothed_full = lax.scan(backward_step, next_full, backward_inputs, reverse=True)[1]
    filtered = lax.dynamic_slice_in_dim(filtered_full, row_start, row_count, 1)
    smoothed = lax.dynamic_slice_in_dim(smoothed_full, row_start, row_count, 1)
    return (filtered, smoothed)


def solution(mesh):
    return jax.shard_map(
        shards,
        mesh=mesh,
        in_specs=(
            P("tm", None),
            P("tm"),
            P(),
            P(("tm", "rows"), None),
            P(("tm", "rows"), None),
            P(),
            P(("tm", "rows"), None),
            P(("tm", "rows"), None),
        ),
        out_specs=(P("tm", "rows"), P("tm", "rows")),
        check_vma=False,
    )
```

profile of v0, /device:TPU:47, one launch (start us, length us, event | category | flops | bytes accessed | tf_op | source)
XLA Modules:
  0.0 942.0 jit_solution(2322415368678451098)
XLA Ops:
  10.1 66.6 %all-gather.21.cloned.1.call-done = f32[1024,1024]{1,0:T(8,128)} async-done(((f32[8,1024]{1,0:T(8,128)}), f32[1024,1024]{1,0:T(8,128)}) %all-gather.21.cloned.1.call-update) | async-done | bytes 4194320 | tf_op jit(solution)/shard_map/all_gather | solution.py:62
  76.7 67.3 %all-gather.23.cloned.1.call-done = f32[1024,1024]{1,0:T(8,128)} async-done(((f32[8,1024]{1,0:T(8,128)}), f32[1024,1024]{1,0:T(8,128)}) %all-gather.23.cloned.1.call-update) | async-done | bytes 4194320 | tf_op jit(solution)/shard_map/all_gather | solution.py:63
  144.1 8.4 pad_maximum_fusion
  152.5 88.6 %while.78 = (s32[]{:T(128)}, f32[128,1024]{0,1:T(8,128)S(1)}, s32[8]{0:T(128)S(1)}, f32[2,1024,1024]{2,1,0:T(8,128)}, s32[]{:T(128)}, /*index=5*/s32[]{:T(128)}, s32[]{:T(128)}, s32[]{:T(128)}) while((s32[]{:T(128)}, f32[128,1024]{0,1:T(8,128)S(1)}, s32[8]{0:T(128)S(1)}, f32[2,1024,1024]{2,1,0:T(8,128)}, s32[]{:T(128)}, /*index=5*/s32[]{:T(128)}, ...), condition=%wide.region_3.4_spmd, body=%wide.region_2.3_spmd.sunk | while | flops 1610612736 | bytes 6291603 | solution.py:92
  155.1 8.5 fusion.111
  166.1 8.5 fusion.111
  177.2 8.5 fusion.111
  188.3 8.5 fusion.111
  199.4 8.5 fusion.111
  210.4 8.5 fusion.111
  221.5 8.5 fusion.111
  232.6 8.5 fusion.111
  245.4 12.4 %collective-permute-done.1 = f32[128,1024]{0,1:T(8,128)S(1)} collective-permute-done((f32[128,1024]{0,1:T(8,128)S(1)}, f32[128,1024]{0,1:T(8,128)S(1)}, u32[]{:S(2)}, u32[]{:S(2)}) %collective-permute-start.1) | collective-permute-done | bytes 524320 | tf_op jit(solution)/shard_map/ppermute | solution.py:13
  258.8 23.6 %all-gather.31.cloned.1.call-done = f32[1024,1024]{1,0:T(8,128)} async-done(((f32[8,1024]{1,0:T(8,128)}), f32[1024,1024]{1,0:T(8,128)}) %all-gather.31.cloned.1.call-update) | async-done | bytes 4194320 | tf_op jit(solution)/shard_map/all_gather | solution.py:64
  282.4 8.4 pad_maximum_fusion.1
  290.8 98.8 %while.80 = (s32[]{:T(128)}, f32[128,1024]{0,1:T(8,128)S(1)}, s32[8]{0:T(128)S(1)}, f32[2,1024,1024]{2,1,0:T(8,128)}, f32[8]{0:T(128)S(1)}, /*index=5*/s32[]{:T(128)}, s32[]{:T(128)}, s32[]{:T(128)}) while((s32[]{:T(128)}, f32[128,1024]{0,1:T(8,128)S(1)}, s32[8]{0:T(128)S(1)}, f32[2,1024,1024]{2,1,0:T(8,128)}, f32[8]{0:T(128)S(1)}, ...), condition=%wide.region_9.10_spmd, body=%wide.region_8.9_spmd.sunk | while | flops 1610743808 | bytes 6292115 | solution.py:103
  294.0 9.4 fusion.117
  306.5 9.1 fusion.117
  318.8 9.1 fusion.117
  331.1 9.1 fusion.117
  343.5 9.1 fusion.117
  355.8 9.1 fusion.117
  368.1 9.1 fusion.117
  380.4 9.1 fusion.117
  392.1 14.7 %collective-permute-done.9 = f32[128,1024]{0,1:T(8,128)S(1)} collective-permute-done((f32[128,1024]{0,1:T(8,128)S(1)}, f32[128,1024]{0,1:T(8,128)S(1)}, u32[]{:S(2)}, u32[]{:S(2)}) %collective-permute-start.9) | collective-permute-done | bytes 524320 | tf_op jit(solution)/shard_map/ppermute | solution.py:13
  407.9 6.7 fusion.54
  416.5 13.8 %collective-permute-done.3 = f32[128,1024]{1,0:T(8,128)S(1)} collective-permute-done((f32[128,1024]{1,0:T(8,128)S(1)}, f32[128,1024]{1,0:T(8,128)S(1)}, u32[]{:S(2)}, u32[]{:S(2)}) %collective-permute-start.3) | collective-permute-done | bytes 524320 | tf_op jit(solution)/shard_map/ppermute | solution.py:13
  436.8 67.1 %while.77 = (s32[]{:T(128)}, f32[1024]{0:T(1024)S(1)}, s32[8]{0:T(128)S(1)}, f32[2,1024,1024]{2,1,0:T(8,128)}, f32[8,1024]{1,0:T(8,128)S(1)}, /*index=5*/s32[]{:T(128)}, s32[]{:T(128)}, s32[]{:T(128)}) while((s32[]{:T(128)}, f32[1024]{0:T(1024)S(1)}, s32[8]{0:T(128)S(1)}, f32[2,1024,1024]{2,1,0:T(8,128)}, f32[8,1024]{1,0:T(8,128)S(1)}, ...), condition=%wide.region_1.2_spmd, body=%wide.region_0.1_spmd.sunk | while | flops 12583941 | bytes 4223115 | solution.py:83
  456.1 6.0 fusion.108
  464.7 5.8 fusion.108
  508.3 12.1 %all-gather = f32[8,1,128]{2,1,0:T(1,128)S(1)} all-gather(f32[1,1,128]{2,1,0:T(1,128)S(1)} %bitcast.297), channel_id=1, replica_groups=mesh['tm'=16,'rows'=8] {'rows'}, dimensions={0}, use_global_device_ids=true | all-gather | bytes 4608 | tf_op jit(solution)/shard_map/all_gather | solution.py:32
  526.6 11.0 %all-gather.1 = f32[8,1,128]{2,1,0:T(1,128)S(1)} all-gather(f32[1,1,128]{2,1,0:T(1,128)S(1)} %bitcast.298), channel_id=1, replica_groups=mesh['tm'=16,'rows'=8] {'rows'}, dimensions={0}, use_global_device_ids=true | all-gather | bytes 4608 | tf_op jit(solution)/shard_map/all_gather | solution.py:32
  541.1 6.7 fusion.57
  551.2 8.4 all-gather.2
  569.0 10.9 %all-gather.3 = f32[8,1,128]{2,1,0:T(1,128)S(1)} all-gather(f32[1,1,128]{2,1,0:T(1,128)S(1)} %bitcast.294), channel_id=1, replica_groups=mesh['tm'=16,'rows'=8] {'rows'}, dimensions={0}, use_global_device_ids=true | all-gather | bytes 4608 | tf_op jit(solution)/shard_map/all_gather | solution.py:18
  584.8 9.0 all-gather.4
  599.8 10.9 %all-gather.5 = f32[8,1,128]{2,1,0:T(1,128)S(1)} all-gather(f32[1,1,128]{2,1,0:T(1,128)S(1)} %bitcast.289), channel_id=1, replica_groups=mesh['tm'=16,'rows'=8] {'rows'}, dimensions={0}, use_global_device_ids=true | all-gather | bytes 4608 | tf_op jit(solution)/shard_map/all_gather | solution.py:18
  610.7 67.1 %while.79 = (s32[]{:T(128)}, f32[1024]{0:T(1024)S(1)}, f32[8,1024]{1,0:T(8,128)S(1)}, s32[8]{0:T(128)S(1)}, f32[2,1024,1024]{2,1,0:T(8,128)}, /*index=5*/f32[8,1024]{1,0:T(8,128)S(1)}, s32[]{:T(128)}, s32[]{:T(128)}, s32[]{:T(128)}) while((s32[]{:T(128)}, f32[1024]{0:T(1024)S(1)}, f32[8,1024]{1,0:T(8,128)S(1)}, s32[8]{0:T(128)S(1)}, ...), condition=%wide.region_5.6_spmd, body=%wide.region_4.5_spmd.sunk | while | flops 12583941 | bytes 4231319 | solution.py:106
  613.1 5.8 fusion.114
  621.6 5.8 fusion.114
  683.5 76.8 %while.82 = (s32[]{:T(128)}, f32[1024]{0:T(1024)S(1)}, f32[8,1024]{1,0:T(8,128)S(1)}, f32[8]{0:T(128)S(1)}, s32[8]{0:T(128)S(1)}, /*index=5*/f32[2,1024,1024]{2,...) while((s32[]{:T(128)}, f32[1024]{0:T(1024)S(1)}, ...), condition=%wide.region_7.8_spmd.clone, body=%wide.region_6.7_spmd.clone.sunk | while | flops 12587015 | bytes 4243657 | solution.py:119
  766.9 8.9 all-gather.6
  782.8 10.9 %all-gather.7 = f32[8,1,128]{2,1,0:T(1,128)S(1)} all-gather(f32[1,1,128]{2,1,0:T(1,128)S(1)} %bitcast.300), channel_id=1, replica_groups=mesh['tm'=16,'rows'=8] {'rows'}, dimensions={0}, use_global_device_ids=true | all-gather | bytes 4608 | tf_op jit(solution)/shard_map/all_gather | solution.py:32
  801.5 8.1 all-gather.8
  814.4 10.9 %all-gather.9 = f32[8,1,128]{2,1,0:T(1,128)S(1)} all-gather(f32[1,1,128]{2,1,0:T(1,128)S(1)} %bitcast.296), channel_id=1, replica_groups=mesh['tm'=16,'rows'=8] {'rows'}, dimensions={0}, use_global_device_ids=true | all-gather | bytes 4608 | tf_op jit(solution)/shard_map/all_gather | solution.py:18
  830.2 9.0 all-gather.10
  846.1 10.9 %all-gather.11 = f32[8,1,128]{2,1,0:T(1,128)S(1)} all-gather(f32[1,1,128]{2,1,0:T(1,128)S(1)} %bitcast.293), channel_id=1, replica_groups=mesh['tm'=16,'rows'=8] {'rows'}, dimensions={0}, use_global_device_ids=true | all-gather | bytes 4608 | tf_op jit(solution)/shard_map/all_gather | solution.py:18
  857.0 77.0 %while.81 = (s32[]{:T(128)}, f32[1024]{0:T(1024)S(1)}, f32[8,1024]{1,0:T(8,128)S(1)}, f32[8,1024]{1,0:T(8,128)S(1)}, f32[8]{0:T(128)S(1)}, /*index=5*/s32[8]{0:T...) while((s32[]{:T(128)}, f32[1024]{0:T(1024)S(1)}, ...), condition=%wide.region_11.12_spmd, body=%wide.region_10.11_spmd.sunk | while | flops 12585990 | bytes 4251851 | solution.py:122
  (305 shorter events, 319.5 us)
Async XLA Ops:
  7.2 424.0 %copy-start = (f32[8,1024]{1,0:T(8,128)S(1)}, f32[8,1024]{1,0:T(8,128)}, u32[]{:S(2)}) copy-start(f32[8,1024]{1,0:T(8,128)} %param.20) | copy-start | bytes 98308
  7.2 69.5 %all-gather.21.cloned.1.call-start = ((), (), s32[]{:S(2)}) async-start(), calls=%async_computation | async-start | bytes 4227072 | tf_op jit(solution)/shard_map/all_gather | solution.py:62
  7.9 136.1 %all-gather.23.cloned.1.call-start = ((), (), s32[]{:S(2)}) async-start(), calls=%async_computation.1 | async-start | bytes 4227072 | tf_op jit(solution)/shard_map/all_gather | solution.py:63
  8.7 250.1 %all-gather.29.cloned.1.call-start = ((), (), s32[]{:S(2)}) async-start(), calls=%async_computation.4 | async-start | bytes 4227072 | tf_op jit(solution)/shard_map/all_gather | solution.py:65
  9.4 273.0 %all-gather.31.cloned.1.call-start = ((), (), s32[]{:S(2)}) async-start(), calls=%async_computation.5 | async-start | bytes 4227072 | tf_op jit(solution)/shard_map/all_gather | solution.py:64
  10.0 397.9 %all-gather.25.cloned.1.call-start = ((), (), s32[]{:S(2)}) async-start(), calls=%async_computation.2 | async-start | bytes 4718592 | tf_op jit(solution)/shard_map/all_gather | solution.py:31
  144.1 8.4 copy-start.6
  241.1 16.7 %collective-permute-start.1 = (f32[128,1024]{0,1:T(8,128)S(1)}, f32[128,1024]{0,1:T(8,128)S(1)}, u32[]{:S(2)}, u32[]{:S(2)}) collective-permute-start(f32[128,1024]{0,1:T(8,128)S(1)} %broadcast_multiply_fusion), channel_id=1, source_target_pairs={{0,8},{8,16},{16,24},{24,32},{32,40},{40,48},{48,56},{56,64},{64,7... | collective-permute-start | bytes 1572872 | tf_op jit(solution)/shard_map/ppermute | solution.py:13
  257.8 0.8 copy-start.4
  258.7 282.4 %all-gather.33.cloned.1.call-start = ((), (), s32[]{:S(2)}) async-start(), calls=%async_computation.6 | async-start | bytes 4718592 | tf_op jit(solution)/shard_map/all_gather | solution.py:31
  389.6 41.6 %copy-start.5 = (f32[1024]{0:T(1024)S(1)}, f32[1024]{0:T(1024)}, u32[]{:S(2)}) copy-start(f32[1024]{0:T(1024)} %param.22) | copy-start | bytes 12292
  389.6 17.2 %collective-permute-start.9 = (f32[128,1024]{0,1:T(8,128)S(1)}, f32[128,1024]{0,1:T(8,128)S(1)}, u32[]{:S(2)}, u32[]{:S(2)}) collective-permute-start(f32[128,1024]{0,1:T(8,128)S(1)} %get-tuple-element.477), channel_id=1, source_target_pairs={{8,0},{16,8},{24,16},{32,24},{40,32},{48,40},{56,48},{64,56},{72,6... | collective-permute-start | bytes 1572872 | tf_op jit(solution)/shard_map/ppermute | solution.py:13
  406.8 0.8 copy-start.2
  407.6 152.0 %all-gather.27.cloned.1.call-start = ((), (), s32[]{:S(2)}) async-start(), calls=%async_computation.3 | async-start | bytes 4718592 | tf_op jit(solution)/shard_map/all_gather | solution.py:31
  414.5 15.7 %collective-permute-start.3 = (f32[128,1024]{1,0:T(8,128)S(1)}, f32[128,1024]{1,0:T(8,128)S(1)}, u32[]{:S(2)}, u32[]{:S(2)}) collective-permute-start(f32[128,1024]{1,0:T(8,128)S(1)} %fusion.54), channel_id=1, source_target_pairs={{0,16},{8,24},{16,32},{24,40},{32,48},{40,56},{48,64},{56,72},{64,... | collective-permute-start | bytes 1572872 | tf_op jit(solution)/shard_map/ppermute | solution.py:13
  430.3 0.8 copy-start.3
  431.1 365.8 %all-gather.35.cloned.1.call-start = ((), (), s32[]{:S(2)}) async-start(), calls=%async_computation.7 | async-start | bytes 4718592 | tf_op jit(solution)/shard_map/all_gather | solution.py:31
  504.0 4.3 collective-permute-start
  520.8 5.8 collective-permute-start.2
  538.0 13.1 %collective-permute-start.4 = (f32[128]{0:T(128)S(1)}, f32[128]{0:T(128)S(1)}, u32[]{:S(2)}, u32[]{:S(2)}) collective-permute-start(f32[128]{0:T(128)S(1)} %fusion.41), channel_id=1, source_target_pairs={{0,32},{8,40},{16,48},{24,56},{32,64},{40,72},{48,80},{56,88},{64,... | collective-permute-start | bytes 1544 | tf_op jit(solution)/shard_map/ppermute | solution.py:13
  547.8 50.9 %collective-permute-start.11 = (f32[128,1024]{1,0:T(8,128)S(1)}, f32[128,1024]{1,0:T(8,128)S(1)}, u32[]{:S(2)}, u32[]{:S(2)}) collective-permute-start(f32[128,1024]{1,0:T(8,128)S(1)} %fusion.57), channel_id=1, source_target_pairs={{16,0},{24,8},{32,16},{40,24},{48,32},{56,40},{64,48},{72,56},{80,... | collective-permute-start | bytes 1572872 | tf_op jit(solution)/shard_map/ppermute | solution.py:13
  564.6 4.4 collective-permute-start.5
  580.4 4.4 collective-permute-start.6
  594.2 5.6 collective-permute-start.7
  598.7 0.8 copy-start.1
  760.4 6.5 collective-permute-start.8
  776.1 6.7 collective-permute-start.10
  794.1 7.3 collective-permute-start.12
  810.0 4.4 collective-permute-start.13
  825.8 4.4 collective-permute-start.14
  839.6 6.5 collective-permute-start.15
Sparse Core Ops, SparseCore 0:
  11.2 65.5 all-gather.20
  79.9 64.1 all-gather.22
  147.2 64.1 all-gather.28
  214.5 67.8 all-gather.30
  283.9 36.1 all-gather.24
  407.7 36.7 all-gather.32
  446.2 32.3 all-gather.26
  599.6 30.8 all-gather.34
where the time goes:
time: 952 us; the launch traced here: 942 us
  matrix products  364 us (38%)
  waiting for transfers between devices  225 us (24%)
  blocking collectives  121 us (13%)
  loops' own time  93.2 us (10%)
  local copies, waits for them, and re-layouts  50.7 us (5%)
  starting transfers between devices  46.2 us (5%)
  other arithmetic  27.2 us (3%)
  between operations  15 us (2%)
    dot_general x16, matrix products, forward_step(): state_vec = precise_dot(matrix, state_vec) + inject_row  92.6 us
    dot_general x16, matrix products, backward_step(): precise_dot(matrix, state_vec - predicted_row)  92.1 us
    all_gather x8, blocking collectives, full_state(): return lax.all_gather(moved, 'rows', axis=0, tiled=True)  78.1 us
    dot_general x8, matrix products, compose_backward(): return (precise_dot(product, matrix) * keep_now, None)  73.3 us
    dot_general x8, matrix products, compose_forward(): return (precise_dot(product, matrix), None)  67.8 us
    all_gather x1, waiting for transfers between devices, shards(): lax.all_gather(closed_loop, ('tm', 'rows'), axis=0, tiled=True)  67.3 us
    all_gather x1, waiting for transfers between devices, shards(): lax.all_gather(transition, ('tm', 'rows'), axis=0, tiled=True)  66.6 us
    ppermute x16, waiting for transfers between devices, shifted(): lax.ppermute(value, axis, [(source, source + steps) for source in range(i...  64.5 us
  transfers between devices with their start and end apart: 24, of which 16 were waited for; matrix products, arithmetic and copies ran while one was open for 40% of the time, Pallas kernels for 0%

commit v1 on v0

--- a/solution.py
+++ b/solution.py
@@ -60,7 +60,12 @@
     row_start = lax.axis_index("rows") * row_count
     trans_full, closed_full, seen_full, missing_full = (
         lax.all_gather(transition, ("tm", "rows"), axis=0, tiled=True),
-        lax.all_gather(closed_loop, ("tm", "rows"), axis=0, tiled=True),
+        jnp.concatenate(
+            lax.all_to_all(
+                jnp.stack([closed_loop] * lax.axis_size(("tm", "rows"))), ("tm", "rows"), 0, 0
+            ),
+            axis=0,
+        ),
         lax.all_gather(smooth_observed, ("tm", "rows"), axis=0, tiled=True),
         lax.all_gather(smooth_missing, ("tm", "rows"), axis=0, tiled=True),
     )

time: 952 us -> 921 us (0.967)
  waiting for transfers between devices: 225 us -> 180 us
  starting transfers between devices: 46.2 us -> 56.7 us
    all_gather x1 -> x0, waiting for transfers between devices: 67.3 us -> none  [shards(): lax.all_gather(closed_loop, ('tm', 'rows'), axis=0, tiled=True)]
    all_to_all x0 -> x1, waiting for transfers between devices: none -> 49 us  [shards(): lax.all_to_all(jnp.stack([closed_loop] * lax.axis_size(('tm', 'rows'))),...]
    all_gather x1, waiting for transfers between devices: 66.6 us -> 40.6 us  [shards(): lax.all_gather(transition, ('tm', 'rows'), axis=0, tiled=True)]
    all_to_all x0 -> x1, starting transfers between devices: none -> 10.9 us  [shards(): lax.all_to_all(jnp.stack([closed_loop] * lax.axis_size(('tm', 'rows'))),...]
  transfers between devices with their start and end apart: 24 -> 24, of which waited for: 16 -> 16; matrix products, arithmetic and copies ran while one was open for 40% -> 42% of each run, Pallas kernels for 0% -> 0%
where the time goes in v1:
time: 921 us; the launch traced here: 909 us
  matrix products  364 us (40%)
  waiting for transfers between devices  180 us (20%)
  blocking collectives  121 us (13%)
  loops' own time  92.2 us (10%)
  starting transfers between devices  56.7 us (6%)
  local copies, waits for them, and re-layouts  53.3 us (6%)
  other arithmetic  26.7 us (3%)
  between operations  15 us (2%)
    dot_general x16, matrix products, forward_step(): state_vec = precise_dot(matrix, state_vec) + inject_row  92.7 us
    dot_general x16, matrix products, backward_step(): precise_dot(matrix, state_vec - predicted_row)  92.1 us
    all_gather x8, blocking collectives, full_state(): return lax.all_gather(moved, 'rows', axis=0, tiled=True)  78.1 us
    dot_general x8, matrix products, compose_backward(): return (precise_dot(product, matrix) * keep_now, None)  73.3 us
    dot_general x8, matrix products, compose_forward(): return (precise_dot(product, matrix), None)  67.9 us
    ppermute x16, waiting for transfers between devices, shifted(): lax.ppermute(value, axis, [(source, source + steps) for source in range(i...  64.8 us
    all_to_all x1, waiting for transfers between devices, shards(): lax.all_to_all(jnp.stack([closed_loop] * lax.axis_size(('tm', 'rows'))),...  49 us
    ppermute x16, starting transfers between devices, shifted(): lax.ppermute(value, axis, [(source, source + steps) for source in range(i...  45.4 us
  transfers between devices with their start and end apart: 24, of which 16 were waited for; matrix products, arithmetic and copies ran while one was open for 42% of the time, Pallas kernels for 0%

profile of v1, /device:TPU:47, one launch (start us, length us, event | category | flops | bytes accessed | tf_op | source)
XLA Modules:
  0.0 909.4 jit_solution(1329519714842135245)
XLA Ops:
  12.7 10.9 %all-to-all-start = ((f32[128,8,1024]{2,1,0:T(8,128)}), f32[128,8,1024]{2,1,0:T(8,128)}, u32[]{:S(2)}, u32[]{:S(2)}) async-start(f32[128,8,1024]{2,1,0:T(8,128)} %stack.13), calls=%async_computation | async-start | bytes 8388608 | tf_op jit(solution)/shard_map/all_to_all | solution.py:64
  23.8 49.0 %all-to-all-done = f32[128,8,1024]{2,1,0:T(8,128)} async-done(((f32[128,8,1024]{2,1,0:T(8,128)}), f32[128,8,1024]{2,1,0:T(8,128)}, u32[]{:S(2)}, u32[]{:S(2)}) %all-to-all-start) | async-done | bytes 4194336 | tf_op jit(solution)/shard_map/all_to_all | solution.py:64
  72.9 40.6 %all-gather.20.cloned.1.call-done = f32[1024,1024]{1,0:T(8,128)} async-done(((f32[8,1024]{1,0:T(8,128)}), f32[1024,1024]{1,0:T(8,128)}) %all-gather.20.cloned.1.call-update) | async-done | bytes 4194320 | tf_op jit(solution)/shard_map/all_gather | solution.py:62
  113.5 8.4 pad_maximum_fusion
  121.8 88.7 %while.78 = (s32[]{:T(128)}, f32[128,1024]{0,1:T(8,128)S(1)}, s32[8]{0:T(128)S(1)}, f32[2,1024,1024]{2,1,0:T(8,128)}, s32[]{:T(128)}, /*index=5*/s32[]{:T(128)}, s32[]{:T(128)}, s32[]{:T(128)}) while((s32[]{:T(128)}, f32[128,1024]{0,1:T(8,128)S(1)}, s32[8]{0:T(128)S(1)}, f32[2,1024,1024]{2,1,0:T(8,128)}, s32[]{:T(128)}, /*index=5*/s32[]{:T(128)}, ...), condition=%wide.region_3.4_spmd, body=%wide.region_2.3_spmd.sunk | while | flops 1610612736 | bytes 6291603 | solution.py:97
  124.4 8.5 fusion.111
  135.5 8.5 fusion.111
  146.6 8.5 fusion.111
  157.7 8.5 fusion.111
  168.8 8.5 fusion.111
  179.9 8.5 fusion.111
  191.0 8.5 fusion.111
  202.0 8.5 fusion.111
  214.9 12.4 %collective-permute-done.1 = f32[128,1024]{0,1:T(8,128)S(1)} collective-permute-done((f32[128,1024]{0,1:T(8,128)S(1)}, f32[128,1024]{0,1:T(8,128)S(1)}, u32[]{:S(2)}, u32[]{:S(2)}) %collective-permute-start.1) | collective-permute-done | bytes 524320 | tf_op jit(solution)/shard_map/ppermute | solution.py:13
  228.2 23.6 %all-gather.28.cloned.1.call-done = f32[1024,1024]{1,0:T(8,128)} async-done(((f32[8,1024]{1,0:T(8,128)}), f32[1024,1024]{1,0:T(8,128)}) %all-gather.28.cloned.1.call-update) | async-done | bytes 4194320 | tf_op jit(solution)/shard_map/all_gather | solution.py:69
  251.9 8.4 pad_maximum_fusion.1
  260.3 98.8 %while.80 = (s32[]{:T(128)}, f32[128,1024]{0,1:T(8,128)S(1)}, s32[8]{0:T(128)S(1)}, f32[2,1024,1024]{2,1,0:T(8,128)}, f32[8]{0:T(128)S(1)}, /*index=5*/s32[]{:T(128)}, s32[]{:T(128)}, s32[]{:T(128)}) while((s32[]{:T(128)}, f32[128,1024]{0,1:T(8,128)S(1)}, s32[8]{0:T(128)S(1)}, f32[2,1024,1024]{2,1,0:T(8,128)}, f32[8]{0:T(128)S(1)}, ...), condition=%wide.region_9.10_spmd, body=%wide.region_8.9_spmd.sunk | while | flops 1610743808 | bytes 6292115 | solution.py:108
  263.5 9.4 %fusion.117 = f32[128,1024]{0,1:T(8,128)S(1)} fusion(f32[128,1024]{0,1:T(8,128)S(1)} %copy.57, f32[2,1024,1024]{2,1,0:T(8,128)} %get-tuple-element.928, s32[]{:T(128)S(6)} %select_n.70, f32[]{:T(128)} %bitcast.249), kind=kOutput, calls=%fused_computation.19.clone.1 | convolution fusion | flops 1610743808 | bytes 5243396 | tf_op jit(solution)/shard_map/while/body/eval_jaxpr/dot_general | solution.py:106
  276.0 9.1 %fusion.117 = f32[128,1024]{0,1:T(8,128)S(1)} fusion(f32[128,1024]{0,1:T(8,128)S(1)} %copy.57, f32[2,1024,1024]{2,1,0:T(8,128)} %get-tuple-element.928, s32[]{:T(128)S(6)} %select_n.70, f32[]{:T(128)} %bitcast.249), kind=kOutput, calls=%fused_computation.19.clone.1 | convolution fusion | flops 1610743808 | bytes 5243396 | tf_op jit(solution)/shard_map/while/body/eval_jaxpr/dot_general | solution.py:106
  288.3 9.1 %fusion.117 = f32[128,1024]{0,1:T(8,128)S(1)} fusion(f32[128,1024]{0,1:T(8,128)S(1)} %copy.57, f32[2,1024,1024]{2,1,0:T(8,128)} %get-tuple-element.928, s32[]{:T(128)S(6)} %select_n.70, f32[]{:T(128)} %bitcast.249), kind=kOutput, calls=%fused_computation.19.clone.1 | convolution fusion | flops 1610743808 | bytes 5243396 | tf_op jit(solution)/shard_map/while/body/eval_jaxpr/dot_general | solution.py:106
  300.6 9.1 %fusion.117 = f32[128,1024]{0,1:T(8,128)S(1)} fusion(f32[128,1024]{0,1:T(8,128)S(1)} %copy.57, f32[2,1024,1024]{2,1,0:T(8,128)} %get-tuple-element.928, s32[]{:T(128)S(6)} %select_n.70, f32[]{:T(128)} %bitcast.249), kind=kOutput, calls=%fused_computation.19.clone.1 | convolution fusion | flops 1610743808 | bytes 5243396 | tf_op jit(solution)/shard_map/while/body/eval_jaxpr/dot_general | solution.py:106
  313.0 9.1 %fusion.117 = f32[128,1024]{0,1:T(8,128)S(1)} fusion(f32[128,1024]{0,1:T(8,128)S(1)} %copy.57, f32[2,1024,1024]{2,1,0:T(8,128)} %get-tuple-element.928, s32[]{:T(128)S(6)} %select_n.70, f32[]{:T(128)} %bitcast.249), kind=kOutput, calls=%fused_computation.19.clone.1 | convolution fusion | flops 1610743808 | bytes 5243396 | tf_op jit(solution)/shard_map/while/body/eval_jaxpr/dot_general | solution.py:106
  325.3 9.1 %fusion.117 = f32[128,1024]{0,1:T(8,128)S(1)} fusion(f32[128,1024]{0,1:T(8,128)S(1)} %copy.57, f32[2,1024,1024]{2,1,0:T(8,128)} %get-tuple-element.928, s32[]{:T(128)S(6)} %select_n.70, f32[]{:T(128)} %bitcast.249), kind=kOutput, calls=%fused_computation.19.clone.1 | convolution fusion | flops 1610743808 | bytes 5243396 | tf_op jit(solution)/shard_map/while/body/eval_jaxpr/dot_general | solution.py:106
  337.6 9.1 %fusion.117 = f32[128,1024]{0,1:T(8,128)S(1)} fusion(f32[128,1024]{0,1:T(8,128)S(1)} %copy.57, f32[2,1024,1024]{2,1,0:T(8,128)} %get-tuple-element.928, s32[]{:T(128)S(6)} %select_n.70, f32[]{:T(128)} %bitcast.249), kind=kOutput, calls=%fused_computation.19.clone.1 | convolution fusion | flops 1610743808 | bytes 5243396 | tf_op jit(solution)/shard_map/while/body/eval_jaxpr/dot_general | solution.py:106
  349.9 9.1 %fusion.117 = f32[128,1024]{0,1:T(8,128)S(1)} fusion(f32[128,1024]{0,1:T(8,128)S(1)} %copy.57, f32[2,1024,1024]{2,1,0:T(8,128)} %get-tuple-element.928, s32[]{:T(128)S(6)} %select_n.70, f32[]{:T(128)} %bitcast.249), kind=kOutput, calls=%fused_computation.19.clone.1 | convolution fusion | flops 1610743808 | bytes 5243396 | tf_op jit(solution)/shard_map/while/body/eval_jaxpr/dot_general | solution.py:106
  361.6 14.7 %collective-permute-done.9 = f32[128,1024]{0,1:T(8,128)S(1)} collective-permute-done((f32[128,1024]{0,1:T(8,128)S(1)}, f32[128,1024]{0,1:T(8,128)S(1)}, u32[]{:S(2)}, u32[]{:S(2)}) %collective-permute-start.9) | collective-permute-done | bytes 524320 | tf_op jit(solution)/shard_map/ppermute | solution.py:13
  377.4 6.7 fusion.54
  386.0 13.8 %collective-permute-done.3 = f32[128,1024]{1,0:T(8,128)S(1)} collective-permute-done((f32[128,1024]{1,0:T(8,128)S(1)}, f32[128,1024]{1,0:T(8,128)S(1)}, u32[]{:S(2)}, u32[]{:S(2)}) %collective-permute-start.3) | collective-permute-done | bytes 524320 | tf_op jit(solution)/shard_map/ppermute | solution.py:13
  406.3 67.2 %while.77 = (s32[]{:T(128)}, f32[1024]{0:T(1024)S(1)}, s32[8]{0:T(128)S(1)}, f32[2,1024,1024]{2,1,0:T(8,128)}, f32[8,1024]{1,0:T(8,128)S(1)}, /*index=5*/s32[]{:T(128)}, s32[]{:T(128)}, s32[]{:T(128)}) while((s32[]{:T(128)}, f32[1024]{0:T(1024)S(1)}, s32[8]{0:T(128)S(1)}, f32[2,1024,1024]{2,1,0:T(8,128)}, f32[8,1024]{1,0:T(8,128)S(1)}, ...), condition=%wide.region_1.2_spmd, body=%wide.region_0.1_spmd.sunk | while | flops 12583941 | bytes 4223115 | solution.py:88
  425.6 6.1 fusion.108
  477.9 12.0 %all-gather = f32[8,1,128]{2,1,0:T(1,128)S(1)} all-gather(f32[1,1,128]{2,1,0:T(1,128)S(1)} %bitcast.296), channel_id=1, replica_groups=mesh['tm'=16,'rows'=8] {'rows'}, dimensions={0}, use_global_device_ids=true | all-gather | bytes 4608 | tf_op jit(solution)/shard_map/all_gather | solution.py:32
  496.2 10.9 %all-gather.1 = f32[8,1,128]{2,1,0:T(1,128)S(1)} all-gather(f32[1,1,128]{2,1,0:T(1,128)S(1)} %bitcast.297), channel_id=1, replica_groups=mesh['tm'=16,'rows'=8] {'rows'}, dimensions={0}, use_global_device_ids=true | all-gather | bytes 4608 | tf_op jit(solution)/shard_map/all_gather | solution.py:32
  510.6 6.7 fusion.57
  520.7 8.4 all-gather.2
  538.5 10.9 %all-gather.3 = f32[8,1,128]{2,1,0:T(1,128)S(1)} all-gather(f32[1,1,128]{2,1,0:T(1,128)S(1)} %bitcast.293), channel_id=1, replica_groups=mesh['tm'=16,'rows'=8] {'rows'}, dimensions={0}, use_global_device_ids=true | all-gather | bytes 4608 | tf_op jit(solution)/shard_map/all_gather | solution.py:18
  554.2 9.0 all-gather.4
  569.4 10.9 %all-gather.5 = f32[8,1,128]{2,1,0:T(1,128)S(1)} all-gather(f32[1,1,128]{2,1,0:T(1,128)S(1)} %bitcast.288), channel_id=1, replica_groups=mesh['tm'=16,'rows'=8] {'rows'}, dimensions={0}, use_global_device_ids=true | all-gather | bytes 4608 | tf_op jit(solution)/shard_map/all_gather | solution.py:18
  580.3 67.2 %while.79 = (s32[]{:T(128)}, f32[1024]{0:T(1024)S(1)}, f32[8,1024]{1,0:T(8,128)S(1)}, s32[8]{0:T(128)S(1)}, f32[2,1024,1024]{2,1,0:T(8,128)}, /*index=5*/f32[8,1024]{1,0:T(8,128)S(1)}, s32[]{:T(128)}, s32[]{:T(128)}, s32[]{:T(128)}) while((s32[]{:T(128)}, f32[1024]{0:T(1024)S(1)}, f32[8,1024]{1,0:T(8,128)S(1)}, s32[8]{0:T(128)S(1)}, ...), condition=%wide.region_5.6_spmd, body=%wide.region_4.5_spmd.sunk | while | flops 12583941 | bytes 4231319 | solution.py:111
  582.7 5.8 fusion.114
  591.2 5.8 fusion.114
  653.1 76.8 %while.82 = (s32[]{:T(128)}, f32[1024]{0:T(1024)S(1)}, f32[8,1024]{1,0:T(8,128)S(1)}, f32[8]{0:T(128)S(1)}, s32[8]{0:T(128)S(1)}, /*index=5*/f32[2,1024,1024]{2,...) while((s32[]{:T(128)}, f32[1024]{0:T(1024)S(1)}, ...), condition=%wide.region_7.8_spmd.clone, body=%wide.region_6.7_spmd.clone.sunk | while | flops 12587015 | bytes 4243657 | solution.py:124
  736.4 8.9 all-gather.6
  752.4 11.0 %all-gather.7 = f32[8,1,128]{2,1,0:T(1,128)S(1)} all-gather(f32[1,1,128]{2,1,0:T(1,128)S(1)} %bitcast.299), channel_id=1, replica_groups=mesh['tm'=16,'rows'=8] {'rows'}, dimensions={0}, use_global_device_ids=true | all-gather | bytes 4608 | tf_op jit(solution)/shard_map/all_gather | solution.py:32
  771.2 8.1 all-gather.8
  784.1 10.9 %all-gather.9 = f32[8,1,128]{2,1,0:T(1,128)S(1)} all-gather(f32[1,1,128]{2,1,0:T(1,128)S(1)} %bitcast.295), channel_id=1, replica_groups=mesh['tm'=16,'rows'=8] {'rows'}, dimensions={0}, use_global_device_ids=true | all-gather | bytes 4608 | tf_op jit(solution)/shard_map/all_gather | solution.py:18
  799.9 9.0 all-gather.10
  815.8 10.9 %all-gather.11 = f32[8,1,128]{2,1,0:T(1,128)S(1)} all-gather(f32[1,1,128]{2,1,0:T(1,128)S(1)} %bitcast.292), channel_id=1, replica_groups=mesh['tm'=16,'rows'=8] {'rows'}, dimensions={0}, use_global_device_ids=true | all-gather | bytes 4608 | tf_op jit(solution)/shard_map/all_gather | solution.py:18
  826.7 74.7 %while.81 = (s32[]{:T(128)}, f32[1024]{0:T(1024)S(1)}, f32[8,1024]{1,0:T(8,128)S(1)}, f32[8,1024]{1,0:T(8,128)S(1)}, f32[8]{0:T(128)S(1)}, /*index=5*/s32[8]{0:T...) while((s32[]{:T(128)}, f32[1024]{0:T(1024)S(1)}, ...), condition=%wide.region_11.12_spmd, body=%wide.region_10.11_spmd.sunk | while | flops 12585990 | bytes 4251851 | solution.py:127
  (305 shorter events, 327.0 us)
Async XLA Ops:
  7.2 393.5 %copy-start = (f32[8,1024]{1,0:T(8,128)S(1)}, f32[8,1024]{1,0:T(8,128)}, u32[]{:S(2)}) copy-start(f32[8,1024]{1,0:T(8,128)} %param.20) | copy-start | bytes 98308
  7.2 106.3 %all-gather.20.cloned.1.call-start = ((), (), s32[]{:S(2)}) async-start(), calls=%async_computation.1 | async-start | bytes 4227072 | tf_op jit(solution)/shard_map/all_gather | solution.py:62
  7.9 220.3 %all-gather.26.cloned.1.call-start = ((), (), s32[]{:S(2)}) async-start(), calls=%async_computation.4 | async-start | bytes 4227072 | tf_op jit(solution)/shard_map/all_gather | solution.py:70
  8.7 243.2 %all-gather.28.cloned.1.call-start = ((), (), s32[]{:S(2)}) async-start(), calls=%async_computation.5 | async-start | bytes 4227072 | tf_op jit(solution)/shard_map/all_gather | solution.py:69
  12.7 60.1 %all-to-all-start = ((f32[128,8,1024]{2,1,0:T(8,128)}), f32[128,8,1024]{2,1,0:T(8,128)}, u32[]{:S(2)}, u32[]{:S(2)}) async-start(f32[128,8,1024]{2,1,0:T(8,128)} %stack.13), calls=%async_computation | async-start | bytes 8388608 | tf_op jit(solution)/shard_map/all_to_all | solution.py:64
  23.6 353.7 %all-gather.22.cloned.1.call-start = ((), (), s32[]{:S(2)}) async-start(), calls=%async_computation.2 | async-start | bytes 4718592 | tf_op jit(solution)/shard_map/all_gather | solution.py:31
  113.5 8.4 copy-start.6
  210.6 16.7 %collective-permute-start.1 = (f32[128,1024]{0,1:T(8,128)S(1)}, f32[128,1024]{0,1:T(8,128)S(1)}, u32[]{:S(2)}, u32[]{:S(2)}) collective-permute-start(f32[128,1024]{0,1:T(8,128)S(1)} %broadcast_multiply_fusion), channel_id=1, source_target_pairs={{0,8},{8,16},{16,24},{24,32},{32,40},{40,48},{48,56},{56,64},{64,7... | collective-permute-start | bytes 1572872 | tf_op jit(solution)/shard_map/ppermute | solution.py:13
  227.3 0.8 copy-start.4
  228.1 282.4 %all-gather.30.cloned.1.call-start = ((), (), s32[]{:S(2)}) async-start(), calls=%async_computation.6 | async-start | bytes 4718592 | tf_op jit(solution)/shard_map/all_gather | solution.py:31
  359.1 41.6 %copy-start.5 = (f32[1024]{0:T(1024)S(1)}, f32[1024]{0:T(1024)}, u32[]{:S(2)}) copy-start(f32[1024]{0:T(1024)} %param.22) | copy-start | bytes 12292
  359.1 17.2 %collective-permute-start.9 = (f32[128,1024]{0,1:T(8,128)S(1)}, f32[128,1024]{0,1:T(8,128)S(1)}, u32[]{:S(2)}, u32[]{:S(2)}) collective-permute-start(f32[128,1024]{0,1:T(8,128)S(1)} %get-tuple-element.477), channel_id=1, source_target_pairs={{8,0},{16,8},{24,16},{32,24},{40,32},{48,40},{56,48},{64,56},{72,6... | collective-permute-start | bytes 1572872 | tf_op jit(solution)/shard_map/ppermute | solution.py:13
  376.3 0.8 copy-start.2
  377.1 152.0 %all-gather.24.cloned.1.call-start = ((), (), s32[]{:S(2)}) async-start(), calls=%async_computation.3 | async-start | bytes 4718592 | tf_op jit(solution)/shard_map/all_gather | solution.py:31
  384.0 15.7 %collective-permute-start.3 = (f32[128,1024]{1,0:T(8,128)S(1)}, f32[128,1024]{1,0:T(8,128)S(1)}, u32[]{:S(2)}, u32[]{:S(2)}) collective-permute-start(f32[128,1024]{1,0:T(8,128)S(1)} %fusion.54), channel_id=1, source_target_pairs={{0,16},{8,24},{16,32},{24,40},{32,48},{40,56},{48,64},{56,72},{64,... | collective-permute-start | bytes 1572872 | tf_op jit(solution)/shard_map/ppermute | solution.py:13
  399.7 0.8 copy-start.3
  400.6 366.0 %all-gather.32.cloned.1.call-start = ((), (), s32[]{:S(2)}) async-start(), calls=%async_computation.7 | async-start | bytes 4718592 | tf_op jit(solution)/shard_map/all_gather | solution.py:31
  473.6 4.3 collective-permute-start
  490.3 5.8 collective-permute-start.2
  507.5 13.2 %collective-permute-start.4 = (f32[128]{0:T(128)S(1)}, f32[128]{0:T(128)S(1)}, u32[]{:S(2)}, u32[]{:S(2)}) collective-permute-start(f32[128]{0:T(128)S(1)} %fusion.41), channel_id=1, source_target_pairs={{0,32},{8,40},{16,48},{24,56},{32,64},{40,72},{48,80},{56,88},{64,... | collective-permute-start | bytes 1544 | tf_op jit(solution)/shard_map/ppermute | solution.py:13
  517.3 50.8 %collective-permute-start.11 = (f32[128,1024]{1,0:T(8,128)S(1)}, f32[128,1024]{1,0:T(8,128)S(1)}, u32[]{:S(2)}, u32[]{:S(2)}) collective-permute-start(f32[128,1024]{1,0:T(8,128)S(1)} %fusion.57), channel_id=1, source_target_pairs={{16,0},{24,8},{32,16},{40,24},{48,32},{56,40},{64,48},{72,56},{80,... | collective-permute-start | bytes 1572872 | tf_op jit(solution)/shard_map/ppermute | solution.py:13
  534.1 4.4 collective-permute-start.5
  549.9 4.4 collective-permute-start.6
  563.7 5.7 collective-permute-start.7
  568.1 0.8 copy-start.1
  730.0 6.4 collective-permute-start.8
  745.7 6.7 collective-permute-start.10
  763.8 7.4 collective-permute-start.12
  779.7 4.4 collective-permute-start.13
  795.5 4.4 collective-permute-start.14
  809.3 6.5 collective-permute-start.15
Sparse Core Ops, SparseCore 0:
  11.2 102.2 all-gather.19
  116.6 64.1 all-gather.25
  184.0 67.8 all-gather.27
  253.4 36.1 all-gather.21
  377.2 36.7 all-gather.29
  415.6 32.3 all-gather.23
  569.1 30.8 all-gather.31
